TPU v7x, 256 devices: a whole 4x4x8 slice. The times are simulated.
256 devices in a mesh: ctx: 128 (over y, x, z), tp: 2 (over core).
Axes of the slice: x: 4, y: 4, z: 8, core: 2. Of those that a mesh axis runs over, the one named last changes fastest.
Arguments:
- hidden: bfloat16 [32768, 4096], P('ctx', 'tp'), may hold values from -6 to 6
- w_query: bfloat16 [4096, 4096], P('ctx', 'tp'), may hold values from -0.09375 to 0.09375
- key_weight: bfloat16 [4096, 256], P('ctx', 'tp'), may hold values from -0.09375 to 0.09375
- value_weight: bfloat16 [4096, 256], P('ctx', 'tp'), may hold values from -0.09375 to 0.09375
- q_gain: float32 [128], replicated, may hold values from 0.5 to 2
- key_norm_gain: float32 [128], replicated, may hold values from 0.5 to 2
- earlier_keys: bfloat16 [131072, 256], P('ctx', 'tp'), may hold values from -288 to 288
- earlier_values: bfloat16 [131072, 256], P('ctx', 'tp'), may hold values from -6 to 6
- counts: int32 [64], replicated, may hold values from 1 to 16, as said below
- place: int32 [64, 16], replicated, may hold values from 0 to 15, as said below
Outputs:
- attended: bfloat16 [32768, 4096], P('ctx', 'tp')
- new_keys: bfloat16 [32768, 256], P('ctx', 'tp')
- new_values: bfloat16 [32768, 256], P('ctx', 'tp')
Inputs may be any that keep to these rules, and one draw needn't show every extreme that they name: `counts`: 16 for one trajectory and 1 for another in every draw; most trajectories have few blocks. `place`: each row orders all 16 slots of the trajectory; the slots after the first counts[b] hold stale data.
All inputs are finite; a program needn't handle non-finite values.
Results may differ from a plain program's by a relative error of at most 0.007.
Values may be sent and summed in bfloat16 or wider, within the bound.
A program may use at most 64 MiB of HBM per device.

v0:
```python
import math
import jax
import jax.numpy as jnp
from jax import lax
from jax.sharding import PartitionSpec as P

HEAD_SIZE = 128
BLOCK_TOKENS = 128


def from_partner(value, axis, apart):
    mask = 2**apart
    pairs = [(source, source ^ mask) for source in range(lax.axis_size(axis))]
    return lax.ppermute(value, axis, pairs)


def normalize_and_turn(values, gain, token_position):
    width = values.shape[-1]
    half = width // 2
    scaled = values * lax.rsqrt(jnp.mean(values * values, axis=-1, keepdims=True) + 1e-06) * gain
    freq = jnp.exp(jnp.arange(half, dtype=jnp.float32) * (-2.0 / width) * math.log(1000000.0))
    angle = token_position.astype(jnp.float32)[:, None] * freq[None, :]
    cosine = jnp.cos(angle)[:, None, :]
    sine = jnp.sin(angle)[:, None, :]
    leading_index = scaled[..., :half]
    second = scaled[..., half:]
    return jnp.concatenate(
        [leading_index * cosine - second * sine, second * cosine + leading_index * sine], axis=-1
    )


def in_order(mine, theirs, lower):
    return jnp.where(
        lower, jnp.concatenate([mine, theirs], axis=0), jnp.concatenate([theirs, mine], axis=0)
    )


def on_device(
    hidden,
    w_query,
    key_weight,
    value_weight,
    q_gain,
    key_norm_gain,
    earlier_keys,
    earlier_values,
    counts,
    place,
):
    lower = lax.axis_index("ctx") % 2 == 0
    traj_id = lax.axis_index("ctx") // 2
    whole = lax.all_gather(hidden, "tp", axis=1, tiled=True)
    tok_rows = whole.shape[0]

    def add_rows(piece):
        return jnp.dot(whole, piece, preferred_element_type=jnp.float32)

    query = add_rows(lax.all_gather(w_query, "ctx", axis=0, tiled=True))
    key_projected = add_rows(lax.all_gather(key_weight, "ctx", axis=0, tiled=True))
    value_projected = add_rows(lax.all_gather(value_weight, "ctx", axis=0, tiled=True))
    heads_q = w_query.shape[1] // HEAD_SIZE
    heads_kv = key_weight.shape[1] // HEAD_SIZE
    count = lax.dynamic_index_in_dim(counts, traj_id, 0, keepdims=False)
    offsets = lax.axis_index("ctx") % 2 * tok_rows + jnp.arange(tok_rows, dtype=jnp.int32)
    token_position = count * BLOCK_TOKENS + offsets
    rotated = normalize_and_turn(
        query.reshape(tok_rows, heads_q, HEAD_SIZE), q_gain, token_position
    ).astype(jnp.bfloat16)
    keys_mine = (
        normalize_and_turn(
            key_projected.reshape(tok_rows, heads_kv, HEAD_SIZE), key_norm_gain, token_position
        )
        .astype(jnp.bfloat16)
        .reshape(tok_rows, heads_kv * HEAD_SIZE)
    )
    values_mine = value_projected.astype(jnp.bfloat16)
    other_ck, other_cv, keys_other, values_other = from_partner(
        (earlier_keys, earlier_values, keys_mine, values_mine), "ctx", 0
    )
    keys_all = jnp.concatenate(
        [in_order(earlier_keys, other_ck, lower), in_order(keys_mine, keys_other, lower)], axis=0
    )
    vals_all = jnp.concatenate(
        [in_order(earlier_values, other_cv, lower), in_order(values_mine, values_other, lower)],
        axis=0,
    )
    slot_total = place.shape[1]
    cache_rows = slot_total * BLOCK_TOKENS
    order = lax.dynamic_index_in_dim(place, traj_id, 0, keepdims=False)
    used = jnp.arange(slot_total, dtype=jnp.int32) < count
    live = jnp.any(
        (order[:, None] == jnp.arange(slot_total, dtype=jnp.int32)[None, :]) & used[:, None], axis=0
    )
    live_tok = jnp.repeat(live, BLOCK_TOKENS)
    stretch_pos = jnp.arange(2 * tok_rows, dtype=jnp.int32)
    query_group = heads_q // heads_kv
    rows_total = query_group * tok_rows
    block_rows = min(rows_total, 512)
    block_count = rows_total // block_rows
    starts = jnp.arange(block_count, dtype=jnp.int32) * block_rows
    query_rows = jnp.transpose(rotated, (1, 0, 2)).reshape(block_count, block_rows, HEAD_SIZE)

    def attend(operands):
        block, begin = operands
        token = (begin + jnp.arange(block_rows, dtype=jnp.int32)) % tok_rows
        own_pos = lax.axis_index("ctx") % 2 * tok_rows + token
        score = lax.dot_general(
            block, keys_all, (((1,), (1,)), ((), ())), preferred_element_type=jnp.float32
        ) * HEAD_SIZE ** (-0.5)
        allowed = jnp.concatenate(
            [
                jnp.broadcast_to(live_tok[None, :], (block_rows, cache_rows)),
                stretch_pos[None, :] <= own_pos[:, None],
            ],
            axis=1,
        )
        score = jnp.where(allowed, score, -jnp.inf)
        top = jnp.max(score, axis=-1, keepdims=True)
        weight = jnp.exp(score - top)
        total = jnp.sum(weight, axis=-1, keepdims=True)
        mixed = (
            jnp.dot(weight.astype(jnp.bfloat16), vals_all, preferred_element_type=jnp.float32)
            / total
        )
        return mixed.astype(jnp.bfloat16)

    result = lax.map(attend, (query_rows, starts))
    outputs = jnp.transpose(result.reshape(query_group, tok_rows, HEAD_SIZE), (1, 0, 2))
    attended = outputs.reshape(tok_rows, heads_q * HEAD_SIZE)
    return (attended, keys_mine, values_mine)


def solution(mesh):
    placed = (
        P("ctx", "tp"),
        P("ctx", "tp"),
        P("ctx", "tp"),
        P("ctx", "tp"),
        P(),
        P(),
        P("ctx", "tp"),
        P("ctx", "tp"),
        P(),
        P(),
    )
    return jax.shard_map(
        on_device,
        mesh=mesh,
        in_specs=placed,
        out_specs=(P("ctx", "tp"), P("ctx", "tp"), P("ctx", "tp")),
        check_vma=False,
    )
```

profile of v0, /device:TPU:1, one launch (start us, length us, event | category | flops | bytes accessed | tf_op | source)
XLA Modules:
  0.0 450.9 jit_solution(13506586590148056657)
XLA Ops:
  7.2 0.7 all-gather.9.cloned.1.call-update
  8.0 0.7 all-gather.5.cloned.1.call-update
  8.7 0.7 all-gather.11.cloned.1.call-update
  10.0 2.6 collective-permute-start
  12.6 1.2 dynamic_slice.25
  15.1 0.7 iota_compare_fusion.2
  16.6 1.2 collective-permute-done
  17.8 1.2 maximum_select_fusion
  19.0 4.4 collective-permute-done.2
  23.6 90.1 %all-gather.9.cloned.1.call-done = bf16[4096,128]{1,0:T(8,128)(2,1)} async-done(((bf16[32,128]{1,0:T(8,128)(2,1)}), bf16[4096,128]{1,0:T(8,128)(2,1)}) %all-gather.9.cloned.1.call-update) | async-done | bytes 1048592 | tf_op jit(solution)/shard_map/all_gather | solution.py:59
  113.7 21.4 %all-gather.5.cloned.1.call-done = bf16[256,4096]{1,0:T(8,128)(2,1)} async-done(((bf16[256,2048]{1,0:T(8,128)(2,1)}), bf16[256,4096]{1,0:T(8,128)(2,1)}) %all-gather.5.cloned.1.call-update) | async-done | bytes 2097168 | tf_op jit(solution)/shard_map/all_gather | solution.py:52
  135.2 2.8 multiply_reduce_fusion.1
  138.0 0.7 multiply_bitcast_fusion
  139.7 1.0 collective-permute-start.1
  140.7 96.9 %all-gather.11.cloned.1.call-done = bf16[4096,128]{1,0:T(8,128)(2,1)} async-done(((bf16[32,128]{1,0:T(8,128)(2,1)}), bf16[4096,128]{1,0:T(8,128)(2,1)}) %all-gather.11.cloned.1.call-update) | async-done | bytes 1048592 | tf_op jit(solution)/shard_map/all_gather | solution.py:60
  237.6 2.1 convolution_convert_fusion
  239.7 1.6 copy.49
  241.3 0.7 copy.50
  242.0 1.2 collective-permute-start.3
  243.2 1.6 maximum_select_fusion.2
  244.8 1.7 copy.45
  246.5 1.6 maximum_select_fusion.3
  248.1 1.7 copy.47
  249.7 1.8 pad_maximum_fusion
  251.5 0.9 pad_maximum_fusion.1
  252.5 141.8 %all-gather.7.cloned.1.call-done = bf16[4096,2048]{1,0:T(8,128)(2,1)} async-done(((bf16[32,2048]{1,0:T(8,128)(2,1)}), bf16[4096,2048]{1,0:T(8,128)(2,1)}) %all-gather.7.cloned.1.call-update) | async-done | bytes 16777232 | tf_op jit(solution)/shard_map/all_gather | solution.py:58
  394.3 8.2 %convolution_bitcast_fusion = f32[32,8,16,128]{3,1,2,0:T(8,128)S(1)} fusion(bf16[256,4096]{1,0:T(8,128)(2,1)S(1)} %copy-done.1, bf16[4096,2048]{1,0:T(8,128)(2,1)} %all-gather.7.cloned.1.call-done), kind=kOutput, calls=%fused_computation.26 | convolution fusion | flops 4294967296 | bytes 20971520 | tf_op jit(solution)/shard_map/dot_general | solution.py:56
  403.7 0.9 multiply_multiply_fusion
  404.6 0.8 subtract_convert_fusion
  406.8 35.5 %while.14 = (s32[]{:T(128)}, bf16[8,512,128]{2,1,0:T(8,128)(2,1)S(1)}, s32[8]{0:T(128)S(1)}, bf16[8,512,128]{2,1,0:T(8,128)(2,1)S(1)}, bf16[2560,128]{1,0:T(8,12...) while((s32[]{:T(128)}, ...), condition=%wide.region_6.7_spmd.clone, body=%wide.region_3.6_spmd.clone.sunk | while | flops 681973248 | bytes 17850196 | solution.py:127
  407.4 0.7 fusion.57
  408.4 1.1 fusion.58
  409.4 0.8 fusion.59
  410.3 1.0 fusion.60
  411.9 0.7 fusion.57
  412.8 1.1 fusion.58
  413.9 0.8 fusion.59
  414.7 1.0 fusion.60
  416.3 0.7 fusion.57
  417.3 1.1 fusion.58
  418.3 0.8 fusion.59
  419.2 1.0 fusion.60
  420.8 0.7 fusion.57
  421.7 1.1 fusion.58
  422.8 0.8 fusion.59
  423.6 1.0 fusion.60
  425.2 0.7 fusion.57
  426.2 1.1 fusion.58
  427.2 0.8 fusion.59
  428.1 1.0 fusion.60
  429.7 0.7 fusion.57
  430.6 1.1 fusion.58
  431.7 0.8 fusion.59
  432.5 1.0 fusion.60
  434.1 0.7 fusion.57
  435.1 1.1 fusion.58
  436.1 0.8 fusion.59
  437.0 1.0 fusion.60
  438.5 0.7 fusion.57
  439.5 1.1 fusion.58
  440.6 0.8 fusion.59
  441.4 1.0 fusion.60
  442.4 0.7 copy.48
  443.1 1.2 copy.55
  (76 shorter events, 12.9 us)
Async XLA Ops:
  7.2 8.6 %copy-start = (s32[64,16]{0,1:T(8,128)S(1)}, s32[64,16]{0,1:T(8,128)}, u32[]{:S(2)}) copy-start(s32[64,16]{0,1:T(8,128)} %param.21) | copy-start | bytes 12292
  7.2 16.3 %copy-start.4 = (bf16[1024,128]{1,0:T(8,128)(2,1)S(1)}, bf16[1024,128]{1,0:T(8,128)(2,1)}, u32[]{:S(2)}) copy-start(bf16[1024,128]{1,0:T(8,128)(2,1)} %param.19) | copy-start | bytes 786436
  7.2 106.5 %all-gather.9.cloned.1.call-start = ((), (), s32[]{:S(2)}) async-start(), calls=%async_computation.2 | async-start | bytes 1056768 | tf_op jit(solution)/shard_map/all_gather | solution.py:59
  7.9 127.2 %all-gather.5.cloned.1.call-start = ((), (), s32[]{:S(2)}) async-start(), calls=%async_computation | async-start | bytes 3145728 | tf_op jit(solution)/shard_map/all_gather | solution.py:52
  8.7 229.0 %all-gather.11.cloned.1.call-start = ((), (), s32[]{:S(2)}) async-start(), calls=%async_computation.3 | async-start | bytes 1056768 | tf_op jit(solution)/shard_map/all_gather | solution.py:60
  9.4 384.9 %all-gather.7.cloned.1.call-start = ((), (), s32[]{:S(2)}) async-start(), calls=%async_computation.1 | async-start | bytes 16908288 | tf_op jit(solution)/shard_map/all_gather | solution.py:58
  10.0 7.8 %collective-permute-start = (bf16[1024,128]{1,0:T(8,128)(2,1)}, bf16[1024,128]{1,0:T(8,128)(2,1)S(1)}, u32[]{:S(2)}, u32[]{:S(2)}) collective-permute-start(bf16[1024,128]{1,0:T(8,128)(2,1)} %param.18), channel_id=1, source_target_pairs={{0,2},{2,0},{4,6},{6,4},{8,10},{10,8},{12,14},{14,12},{16,18},{18,... | collective-permute-start | bytes 786440 | tf_op jit(solution)/shard_map/ppermute | solution.py:14
  12.5 10.9 %collective-permute-start.2 = (bf16[1024,128]{1,0:T(8,128)(2,1)}, bf16[1024,128]{1,0:T(8,128)(2,1)S(1)}, u32[]{:S(2)}, u32[]{:S(2)}) collective-permute-start(bf16[1024,128]{1,0:T(8,128)(2,1)} %param.19), channel_id=1, source_target_pairs={{0,2},{2,0},{4,6},{6,4},{8,10},{10,8},{12,14},{14,12},{16,18},{18,... | collective-permute-start | bytes 786440 | tf_op jit(solution)/shard_map/ppermute | solution.py:14
  14.5 4.5 copy-start.5
  135.2 3.6 copy-start.6
  135.2 102.5 %copy-start.1 = (bf16[256,4096]{1,0:T(8,128)(2,1)S(1)}, bf16[256,4096]{1,0:T(8,128)(2,1)}, u32[]{:S(2)}) copy-start(bf16[256,4096]{1,0:T(8,128)(2,1)} %all-gather.5.cloned.1.call-done) | copy-start | bytes 6291460
  139.7 103.5 %collective-permute-start.1 = (bf16[256,128]{0,1:T(8,128)(2,1)}, bf16[256,128]{0,1:T(8,128)(2,1)}, u32[]{:S(2)}, u32[]{:S(2)}) collective-permute-start(bf16[256,128]{0,1:T(8,128)(2,1)} %pad_maximum_fusion.2), channel_id=1, source_target_pairs={{0,2},{2,0},{4,6},{6,4},{8,10},{10,8},{12,14},{14,12},{16,18},{18,... | collective-permute-start | bytes 196616 | tf_op jit(solution)/shard_map/ppermute | solution.py:14
  242.0 4.4 collective-permute-start.3
  402.9 0.8 copy-start.7
  405.4 1.2 copy-start.2
  405.4 1.4 copy-start.3
  405.4 1.4 copy-start.8
Sparse Core Ops, SparseCore 0:
  11.4 102.2 all-gather.8
  115.5 19.6 all-gather.4
  138.6 99.0 all-gather.10
  241.1 153.1 all-gather.6
where the time goes:
time: 451 us
  waiting for transfers between devices  358 us (79%)
  matrix products  29.2 us (6%)
  other arithmetic  27.5 us (6%)
  local copies, waits for them, and re-layouts  15.7 us (3%)
  between operations  14.7 us (3%)
  starting transfers between devices  4.99 us (1%)
    all_gather x1, waiting for transfers between devices, on_device(): query = add_rows(lax.all_gather(w_query, 'ctx', axis=0, tiled=True))  142 us
    all_gather x1, waiting for transfers between devices, on_device(): lax.all_gather(value_weight, 'ctx', axis=0, tiled=True)  96.9 us
    all_gather x1, waiting for transfers between devices, on_device(): lax.all_gather(key_weight, 'ctx', axis=0, tiled=True)  90.1 us
    all_gather x1, waiting for transfers between devices, on_device(): whole = lax.all_gather(hidden, 'tp', axis=1, tiled=True)  21.4 us
    dot_general x3, matrix products, add_rows(): return jnp.dot(whole, piece, preferred_element_type=jnp.float32)  13.1 us
  transfers between devices with their start and end apart: 8, of which 6 were waited for; matrix products, arithmetic and copies ran while one was open for 5% of the time, Pallas kernels for 0%

commit v1 on v0

--- a/solution.py
+++ b/solution.py
@@ -6,6 +6,13 @@
 
 HEAD_SIZE = 128
 BLOCK_TOKENS = 128
+
+
+def all_by_exchange(block, axis, along):
+    size = lax.axis_size(axis)
+    shards = jnp.stack([block for _ in range(size)])
+    shards = lax.all_to_all(shards, axis, split_axis=0, concat_axis=0)
+    return jnp.concatenate(shards, axis=along)
 
 
 def from_partner(value, axis, apart):
@@ -57,7 +64,7 @@
 
     query = add_rows(lax.all_gather(w_query, "ctx", axis=0, tiled=True))
     key_projected = add_rows(lax.all_gather(key_weight, "ctx", axis=0, tiled=True))
-    value_projected = add_rows(lax.all_gather(value_weight, "ctx", axis=0, tiled=True))
+    value_projected = add_rows(all_by_exchange(value_weight, "ctx", 0))
     heads_q = w_query.shape[1] // HEAD_SIZE
     heads_kv = key_weight.shape[1] // HEAD_SIZE
     count = lax.dynamic_index_in_dim(counts, traj_id, 0, keepdims=False)

time: 451 us -> 349 us (0.77)
  waiting for transfers between devices: 358 us -> 241 us
  starting transfers between devices: 4.99 us -> 20 us
    all_gather x1 -> x0, waiting for transfers between devices: 96.9 us -> none  [on_device(): lax.all_gather(value_weight, 'ctx', axis=0, tiled=True)]
    all_to_all x0 -> x1, starting transfers between devices: none -> 15.8 us  [all_by_exchange(): shards = lax.all_to_all(shards, axis, split_axis=0, concat_axis=0)]
    all_gather x1, waiting for transfers between devices: 90.1 us -> 82.6 us  [on_device(): lax.all_gather(key_weight, 'ctx', axis=0, tiled=True)]
    all_gather x1, waiting for transfers between devices: 142 us -> 135 us  [on_device(): query = add_rows(lax.all_gather(w_query, 'ctx', axis=0, tiled=True))]
    ppermute x4, waiting for transfers between devices: 5.59 us -> 0.01 us  [from_partner(): return lax.ppermute(value, axis, pairs)]
  transfers between devices with their start and end apart: 8 -> 8, of which waited for: 6 -> 3; matrix products, arithmetic and copies ran while one was open for 5% -> 7% of each run, Pallas kernels for 0% -> 0%
where the time goes in v1:
time: 349 us; the launch traced here: 348 us
  waiting for transfers between devices  241 us (69%)
  matrix products  29.2 us (8%)
  other arithmetic  26.5 us (8%)
  starting transfers between devices  20 us (6%)
  local copies, waits for them, and re-layouts  16.9 us (5%)
  between operations  14.7 us (4%)
    all_gather x1, waiting for transfers between devices, on_device(): query = add_rows(lax.all_gather(w_query, 'ctx', axis=0, tiled=True))  135 us
    all_gather x1, waiting for transfers between devices, on_device(): lax.all_gather(key_weight, 'ctx', axis=0, tiled=True)  82.6 us
    all_gather x1, waiting for transfers between devices, on_device(): whole = lax.all_gather(hidden, 'tp', axis=1, tiled=True)  21.4 us
    all_to_all x1, starting transfers between devices, all_by_exchange(): shards = lax.all_to_all(shards, axis, split_axis=0, concat_axis=0)  15.8 us
    dot_general x3, matrix products, add_rows(): return jnp.dot(whole, piece, preferred_element_type=jnp.float32)  13.1 us
    dot_general x8, matrix products, attend(): lax.dot_general(block, keys_all, (((1,), (1,)), ((), ())), preferred_elem...  8.42 us
    dot_general x8, matrix products, attend(): jnp.dot(weight.astype(jnp.bfloat16), vals_all, preferred_element_type=jnp...  7.71 us
  transfers between devices with their start and end apart: 8, of which 3 were waited for; matrix products, arithmetic and copies ran while one was open for 7% of the time, Pallas kernels for 0%

profile of v1, /device:TPU:1, one launch (start us, length us, event | category | flops | bytes accessed | tf_op | source)
XLA Modules:
  0.0 348.3 jit_solution(1175248514359856489)
XLA Ops:
  7.2 0.7 all-gather.8.cloned.1.call-update
  8.0 0.7 all-gather.4.cloned.1.call-update
  8.7 0.7 all-gather.6.cloned.1.call-update
  9.4 2.6 collective-permute-start
  12.1 1.8 stack.2
  13.9 15.8 %all-to-all-start = ((bf16[128,32,128]{2,1,0:T(8,128)(2,1)}), bf16[128,32,128]{2,1,0:T(8,128)(2,1)}, u32[]{:S(2)}, u32[]{:S(2)}) async-start(bf16[128,32,128]{2,1,0:T(8,128)(2,1)} %stack.2), calls=%async_computation | async-start | bytes 2097152 | tf_op jit(solution)/shard_map/all_to_all | solution.py:14
  29.7 0.6 dynamic_slice.25
  31.5 0.7 iota_compare_fusion.2
  33.4 82.6 %all-gather.8.cloned.1.call-done = bf16[4096,128]{1,0:T(8,128)(2,1)} async-done(((bf16[32,128]{1,0:T(8,128)(2,1)}), bf16[4096,128]{1,0:T(8,128)(2,1)}) %all-gather.8.cloned.1.call-update) | async-done | bytes 1048592 | tf_op jit(solution)/shard_map/all_gather | solution.py:66
  116.0 21.4 %all-gather.4.cloned.1.call-done = bf16[256,4096]{1,0:T(8,128)(2,1)} async-done(((bf16[256,2048]{1,0:T(8,128)(2,1)}), bf16[256,4096]{1,0:T(8,128)(2,1)}) %all-gather.4.cloned.1.call-update) | async-done | bytes 2097168 | tf_op jit(solution)/shard_map/all_gather | solution.py:59
  137.4 2.8 multiply_reduce_fusion.1
  140.3 0.7 multiply_bitcast_fusion
  141.4 0.6 pad_maximum_fusion.2
  142.0 1.0 collective-permute-start.1
  143.0 2.1 convolution_convert_fusion
  145.1 1.6 copy.49
  146.7 0.7 copy.50
  147.9 1.6 maximum_select_fusion.2
  149.5 1.7 copy.45
  151.1 1.6 maximum_select_fusion.3
  152.7 1.7 copy.47
  154.4 1.8 pad_maximum_fusion
  156.2 0.9 pad_maximum_fusion.1
  157.1 134.6 %all-gather.6.cloned.1.call-done = bf16[4096,2048]{1,0:T(8,128)(2,1)} async-done(((bf16[32,2048]{1,0:T(8,128)(2,1)}), bf16[4096,2048]{1,0:T(8,128)(2,1)}) %all-gather.6.cloned.1.call-update) | async-done | bytes 16777232 | tf_op jit(solution)/shard_map/all_gather | solution.py:65
  291.8 8.2 %convolution_bitcast_fusion = f32[32,8,16,128]{3,1,2,0:T(8,128)S(1)} fusion(bf16[256,4096]{1,0:T(8,128)(2,1)S(1)} %copy-done.1, bf16[4096,2048]{1,0:T(8,128)(2,1)} %all-gather.6.cloned.1.call-done), kind=kOutput, calls=%fused_computation.26 | convolution fusion | flops 4294967296 | bytes 20971520 | tf_op jit(solution)/shard_map/dot_general | solution.py:63
  300.4 0.6 multiply_reduce_fusion
  301.2 0.9 multiply_multiply_fusion
  302.1 0.8 subtract_convert_fusion
  304.3 35.5 %while.14 = (s32[]{:T(128)}, bf16[8,512,128]{2,1,0:T(8,128)(2,1)S(1)}, s32[8]{0:T(128)S(1)}, bf16[8,512,128]{2,1,0:T(8,128)(2,1)S(1)}, bf16[2560,128]{1,0:T(8,12...) while((s32[]{:T(128)}, ...), condition=%wide.region_6.7_spmd.clone, body=%wide.region_3.6_spmd.clone.sunk | while | flops 681973248 | bytes 17850196 | solution.py:134
  304.9 0.7 fusion.57
  305.9 1.1 fusion.58
  306.9 0.8 fusion.59
  307.8 1.0 fusion.60
  308.8 0.6 dynamic_slice.38
  309.3 0.7 fusion.57
  310.3 1.1 fusion.58
  311.4 0.8 fusion.59
  312.2 1.0 fusion.60
  313.8 0.7 fusion.57
  314.8 1.1 fusion.58
  315.8 0.8 fusion.59
  316.7 1.0 fusion.60
  318.2 0.7 fusion.57
  319.2 1.1 fusion.58
  320.3 0.8 fusion.59
  321.1 1.0 fusion.60
  322.7 0.7 fusion.57
  323.6 1.1 fusion.58
  324.7 0.8 fusion.59
  325.5 1.0 fusion.60
  327.1 0.7 fusion.57
  328.1 1.1 fusion.58
  329.1 0.8 fusion.59
  330.0 1.0 fusion.60
  331.6 0.7 fusion.57
  332.5 1.1 fusion.58
  333.6 0.8 fusion.59
  334.4 1.0 fusion.60
  336.0 0.7 fusion.57
  337.0 1.1 fusion.58
  338.0 0.8 fusion.59
  338.9 1.0 fusion.60
  339.9 0.7 copy.48
  340.5 1.2 copy.55
  (80 shorter events, 11.1 us)
Async XLA Ops:
  7.2 25.0 %copy-start = (s32[64,16]{0,1:T(8,128)S(1)}, s32[64,16]{0,1:T(8,128)}, u32[]{:S(2)}) copy-start(s32[64,16]{0,1:T(8,128)} %param.21) | copy-start | bytes 12292
  7.2 108.8 %all-gather.8.cloned.1.call-start = ((), (), s32[]{:S(2)}) async-start(), calls=%async_computation.3 | async-start | bytes 1056768 | tf_op jit(solution)/shard_map/all_gather | solution.py:66
  7.9 21.8 %copy-start.9 = (s32[64]{0:T(128)S(1)}, s32[64]{0:T(128)}, u32[]{:S(2)}) copy-start(s32[64]{0:T(128)} %param.20) | copy-start | bytes 772
  7.9 25.1 %copy-start.4 = (bf16[1024,128]{1,0:T(8,128)(2,1)S(1)}, bf16[1024,128]{1,0:T(8,128)(2,1)}, u32[]{:S(2)}) copy-start(bf16[1024,128]{1,0:T(8,128)(2,1)} %param.18) | copy-start | bytes 786436
  7.9 129.5 %all-gather.4.cloned.1.call-start = ((), (), s32[]{:S(2)}) async-start(), calls=%async_computation.1 | async-start | bytes 3145728 | tf_op jit(solution)/shard_map/all_gather | solution.py:59
  8.7 283.1 %all-gather.6.cloned.1.call-start = ((), (), s32[]{:S(2)}) async-start(), calls=%async_computation.2 | async-start | bytes 16908288 | tf_op jit(solution)/shard_map/all_gather | solution.py:65
  9.4 23.8 %copy-start.5 = (bf16[1024,128]{1,0:T(8,128)(2,1)S(1)}, bf16[1024,128]{1,0:T(8,128)(2,1)}, u32[]{:S(2)}) copy-start(bf16[1024,128]{1,0:T(8,128)(2,1)} %param.19) | copy-start | bytes 786436
  9.4 23.6 %collective-permute-start = (bf16[1024,128]{1,0:T(8,128)(2,1)}, bf16[1024,128]{1,0:T(8,128)(2,1)S(1)}, u32[]{:S(2)}, u32[]{:S(2)}) collective-permute-start(bf16[1024,128]{1,0:T(8,128)(2,1)} %param.18), channel_id=1, source_target_pairs={{0,2},{2,0},{4,6},{6,4},{8,10},{10,8},{12,14},{14,12},{16,18},{18,... | collective-permute-start | bytes 786440 | tf_op jit(solution)/shard_map/ppermute | solution.py:21
  12.0 21.2 %collective-permute-start.2 = (bf16[1024,128]{1,0:T(8,128)(2,1)}, bf16[1024,128]{1,0:T(8,128)(2,1)S(1)}, u32[]{:S(2)}, u32[]{:S(2)}) collective-permute-start(bf16[1024,128]{1,0:T(8,128)(2,1)} %param.19), channel_id=1, source_target_pairs={{0,2},{2,0},{4,6},{6,4},{8,10},{10,8},{12,14},{14,12},{16,18},{18,... | collective-permute-start | bytes 786440 | tf_op jit(solution)/shard_map/ppermute | solution.py:21
  13.9 129.1 %all-to-all-start = ((bf16[128,32,128]{2,1,0:T(8,128)(2,1)}), bf16[128,32,128]{2,1,0:T(8,128)(2,1)}, u32[]{:S(2)}, u32[]{:S(2)}) async-start(bf16[128,32,128]{2,1,0:T(8,128)(2,1)} %stack.2), calls=%async_computation | async-start | bytes 2097152 | tf_op jit(solution)/shard_map/all_to_all | solution.py:14
  31.0 85.0 %copy-start.6 = (f32[64]{0:T(128)}, f32[64]{0:T(128)S(1)}, u32[]{:S(2)}) copy-start(f32[64]{0:T(128)S(1)} %multiply_exponential_fusion) | copy-start | bytes 772
  137.4 3.6 %copy-start.7 = (f32[64]{0:T(128)S(1)}, f32[64]{0:T(128)}, u32[]{:S(2)}) copy-start(f32[64]{0:T(128)} %copy-done.6) | copy-start | bytes 772
  137.4 5.6 %copy-start.1 = (bf16[256,4096]{1,0:T(8,128)(2,1)S(1)}, bf16[256,4096]{1,0:T(8,128)(2,1)}, u32[]{:S(2)}) copy-start(bf16[256,4096]{1,0:T(8,128)(2,1)} %all-gather.4.cloned.1.call-done) | copy-start | bytes 6291460
  142.0 5.9 %collective-permute-start.1 = (bf16[256,128]{0,1:T(8,128)(2,1)}, bf16[256,128]{0,1:T(8,128)(2,1)}, u32[]{:S(2)}, u32[]{:S(2)}) collective-permute-start(bf16[256,128]{0,1:T(8,128)(2,1)} %pad_maximum_fusion.2), channel_id=1, source_target_pairs={{0,2},{2,0},{4,6},{6,4},{8,10},{10,8},{12,14},{14,12},{16,18},{18,... | collective-permute-start | bytes 196616 | tf_op jit(solution)/shard_map/ppermute | solution.py:21
  147.4 3.7 %collective-permute-start.3 = (bf16[256,128]{0,1:T(8,128)(2,1)S(1)}, bf16[256,128]{0,1:T(8,128)(2,1)}, u32[]{:S(2)}, u32[]{:S(2)}) collective-permute-start(bf16[256,128]{0,1:T(8,128)(2,1)S(1)} %convolution_convert_fusion), channel_id=1, source_target_pairs={{0,2},{2,0},{4,6},{6,4},{8,10},{10,8},{12,14},{14,12},{16,18},{18,... | collective-permute-start | bytes 196616 | tf_op jit(solution)/shard_map/ppermute | solution.py:21
  300.4 0.8 copy-start.8
  302.9 1.2 copy-start.2
  302.9 1.4 copy-start.3
  302.9 1.4 copy-start.10
Sparse Core Ops, SparseCore 0:
  11.4 104.4 all-gather.7
  117.8 19.6 all-gather.3
  141.1 150.6 all-gather.5
